TPU v7x, 256 devices: a whole 4x4x8 slice. The times are simulated.
256 devices in a mesh: sta: 64 (over x_lo, z, y), tpl: 4 (over x_hi, core).
Axes of the slice: x: 4 (x_hi: 2, x_lo: 2; x = x_hi * 2 + x_lo), y: 4, z: 8, core: 2. Of those that a mesh axis runs over, the one named last changes fastest.
Arguments:
- waveform: float32 [128, 1536], P('sta', 'tpl'), may hold values from -6 to 6
- fir_taps: float32 [64], replicated, may hold values from -0.75 to 0.75
- templates: bfloat16 [512, 128, 1024], P('tpl', 'sta'), may hold values from -6 to 6
- presence: int32 [512, 128], P('tpl', 'sta'), may hold values from 0 to 1
- moveout: int32 [512, 128], P('tpl', 'sta'), may hold values from 0 to 128
Outputs:
- network_stack: float32 [4, 128, 384], P('tpl', 'sta')
All inputs are finite; a program needn't handle non-finite values.
Results may differ from a plain program's by a relative error of at most 0.0029.
Values may be sent and summed in bfloat16 or wider, within the bound.
A program may use at most 64 MiB of HBM per device.

v0:
```python
import functools

import jax
import jax.numpy as jnp
from jax import lax
from jax.experimental import pallas as pl
from jax.experimental.pallas import tpu as pltpu
from jax.sharding import PartitionSpec as P

BLK = 128
SHIFT_MOST = 128
ROWS = 8
EPSILON = 1e-06
MESH = pl.DeviceIdType.MESH


def lane_gather(values, index):
    return lax.gather(
        values,
        index[..., None],
        lax.GatherDimensionNumbers(
            offset_dims=(),
            collapsed_slice_dims=(1,),
            start_index_map=(1,),
            operand_batching_dims=(0,),
            start_indices_batching_dims=(0,),
        ),
        slice_sizes=(1, 1),
        mode=lax.GatherScatterMode.PROMISE_IN_BOUNDS,
    )


def split3(values):
    high = values.astype(jnp.bfloat16)
    rest = values - high.astype(jnp.float32)
    middle = rest.astype(jnp.bfloat16)
    low = (rest - middle.astype(jnp.float32)).astype(jnp.bfloat16)
    return [high, middle, low]


def sta_dims(n_sta):
    return {64: (2, 8, 4), 8: (2, 2, 2), 4: (2, 2, 1)}.get(n_sta, (1, n_sta, 1))


def places(me, dims):
    x, rest = me // (dims[1] * dims[2]), me % (dims[1] * dims[2])
    z, y = rest // dims[2], rest % dims[2]
    xs = [((x + d) % dims[0]) * (dims[1] * dims[2]) for d in range(dims[0])]
    ys = [(y + d) % dims[2] for d in range(dims[2])]
    return z, lambda dx, dy, at: xs[dx] + ys[dy] + at * dims[2]


def nearest(z, planes, n):
    return min(planes, key=lambda p: min((z - p) % n, (p - z) % n))


def kernel(
    n_sta,
    n_tpl,
    wave_ref,
    fir_hbm,
    tpl_ref,
    pres_hbm,
    mov_hbm,
    recv_buf,
    wave_buf,
    tpl_raw,
    rows32,
    tpl_split,
    raw_buf,
    filtered_buf,
    edge_buf,
    scale_buf,
    moved_ref,
    weight_ref,
    send_buf,
    taps_ref,
    fir_ref,
    pres_ref,
    mov_ref,
    local_sem,
    small_sem,
    chain_sem,
    wave_send,
    wave_recv,
    stack_send,
    stack_recv,
):
    me_s, me_t = lax.axis_index("sta"), lax.axis_index("tpl")
    dims = sta_dims(n_sta)
    me_z, place = places(me_s, dims)
    early = list(range(max(1, 3 * dims[1] // 8)))
    late = list(range(len(early), dims[1]))
    plane = [(dx, dy) for dx in range(dims[0]) for dy in range(dims[2])]
    plane.sort(key=lambda step: -sum(min(d, n - d) for d, n in zip(step, (dims[0], dims[2]))))
    is_early = me_z < len(early)
    stations = wave_ref.shape[0]
    n_rows = tpl_ref.shape[0]
    lag_blocks = tpl_ref.shape[2] // BLK
    own_rows = n_rows // n_sta
    seg_blocks = wave_ref.shape[1] // BLK
    wave_blocks = seg_blocks * n_tpl
    time_blocks = wave_blocks - lag_blocks
    out_blocks = time_blocks - 1

    def each(planes, do):
        for step in plane:
            for at in planes:
                to = place(*step, at)
                if step == (0, 0):
                    pl.when(me_z != at)(functools.partial(do, to))
                else:
                    do(to)

    def tell(sem, to):
        pl.semaphore_signal(sem, inc=1, device_id={"sta": to}, device_id_type=MESH)

    barrier = pltpu.get_barrier_semaphore()
    for step in range(n_tpl - 1, 0, -1):
        pl.semaphore_signal(barrier, inc=1, device_id={"tpl": lax.rem(me_t + step, n_tpl)}, device_id_type=MESH)

    @pl.when(is_early)
    def _():
        each(late + early, functools.partial(tell, barrier))

    own_wave = pltpu.make_async_copy(wave_ref, wave_buf.at[me_t], local_sem.at[0])
    own_wave.start()
    small_copies = [
        pltpu.make_async_copy(mov_hbm, mov_ref, small_sem.at[0]),
        pltpu.make_async_copy(pres_hbm, pres_ref, small_sem.at[1]),
        pltpu.make_async_copy(fir_hbm, fir_ref, small_sem.at[2]),
    ]
    for copy in small_copies:
        copy.start()
    tpl_copies = []
    for b in range(lag_blocks):
        tpl_copies.append(
            pltpu.make_async_copy(
                tpl_ref.at[:, :, pl.ds(b * BLK, BLK)], tpl_raw.at[b], local_sem.at[1 + b]
            )
        )
        tpl_copies[-1].start()

    n_early = len(plane) * len(early)
    pl.semaphore_wait(barrier, n_tpl - 1 + n_early - is_early.astype(jnp.int32))
    own_wave.wait()
    half = n_tpl // 2
    core = lax.rem(me_t, 2)
    across = lax.rem(me_t - core + half, n_tpl)
    wave_copies = [
        pltpu.make_async_remote_copy(
            src_ref=wave_buf.at[me_t],
            dst_ref=wave_buf.at[me_t],
            send_sem=wave_send.at[k],
            recv_sem=wave_recv.at[sem],
            device_id={"tpl": to},
            device_id_type=MESH,
        )
        for k, (to, sem) in enumerate(((across + 1, 1 + core), (across, 1 + core), (me_t + 1 - 2 * core, 0)))
    ]
    for copy in wave_copies:
        copy.start()

    def wave_wait(sem):
        pltpu.make_async_copy(wave_buf.at[0], wave_buf.at[0], wave_recv.at[sem]).wait()

    @pl.when(jnp.logical_not(is_early))
    def _():
        each(early, functools.partial(tell, chain_sem.at[0]))


    row_view = tpl_raw.reshape(lag_blocks, n_rows * stations, BLK)
    squares = [jnp.zeros((n_rows, BLK), jnp.float32) for _ in range(stations)]
    for b in range(lag_blocks):
        tpl_copies[b].wait()
        rows32[b % 2] = row_view[b].astype(jnp.float32)
        for s in range(stations):
            part = rows32[b % 2, pl.ds(s, n_rows, stride=stations), :]
            squares[s] = squares[s] + part * part
            tpl_split[s, lag_blocks // 2 - 1 - b // 2, :, (b % 2) * BLK : (b % 2 + 1) * BLK] = part.astype(
                jnp.bfloat16
            )

    for copy in small_copies:
        copy.wait()
    taps = jnp.concatenate([fir_ref[...], jnp.zeros((1, BLK - fir_ref.shape[1]), jnp.float32)], axis=1)
    from_at = lax.broadcasted_iota(jnp.int32, (BLK, BLK), 0)
    to_at = lax.broadcasted_iota(jnp.int32, (BLK, BLK), 1)
    turned = lane_gather(jnp.broadcast_to(taps, (BLK, BLK)), (to_at - from_at) & (BLK - 1))
    matrix = jnp.concatenate(
        [jnp.where(to_at >= from_at, turned, 0.0), jnp.where(to_at >= from_at, 0.0, turned)], axis=0
    )
    taps_ref[...] = jnp.concatenate(split3(matrix), axis=1)
    for s in range(stations):
        norm = jnp.sqrt(jnp.sum(squares[s], axis=1, keepdims=True) + EPSILON)
        moved = jnp.transpose(jnp.broadcast_to(mov_ref[s : s + 1, :], (BLK, n_rows)))
        present = jnp.transpose(jnp.broadcast_to(pres_ref[s : s + 1, :].astype(jnp.float32), (BLK, n_rows)))
        weight_ref[s] = present / norm
        moved_ref[s] = moved

    def piece(c):
        return wave_buf[c // seg_blocks, :, (c % seg_blocks) * BLK : (c % seg_blocks + 1) * BLK]

    def filter_blocks(low, high):
        pieces = [piece(c) for c in range(low, high)]
        now = jnp.concatenate(pieces, axis=0)
        first = piece(low - 1) if low else jnp.zeros((stations, BLK), jnp.float32)
        before = jnp.concatenate([first] + pieces[:-1], axis=0)
        parts = split3(jnp.concatenate([now, before], axis=1))
        n = now.shape[0]
        products = jnp.dot(jnp.concatenate(parts, axis=0), taps_ref[...], preferred_element_type=jnp.float32)
        filtered = jnp.zeros((n, BLK), jnp.float32)
        for total in (2, 1, 0):
            for i in range(total + 1):
                filtered = filtered + products[i * n : (i + 1) * n, (total - i) * BLK : (total - i + 1) * BLK]
        return filtered.astype(jnp.bfloat16).astype(jnp.float32)

    def scales_of(filtered):
        power = filtered * filtered
        high = power.astype(jnp.bfloat16)
        low = (power - high.astype(jnp.float32)).astype(jnp.bfloat16)
        taken = lax.broadcasted_iota(jnp.int32, (BLK, BLK), 0)
        at = lax.broadcasted_iota(jnp.int32, (BLK, BLK), 1)
        rest = jnp.where(taken >= at, 1.0, 0.0)
        masks = jnp.concatenate([rest, 1.0 - rest, jnp.ones((BLK, BLK), jnp.float32)], axis=1)
        sums = jnp.dot(
            jnp.concatenate([high, low], axis=0), masks.astype(jnp.bfloat16), preferred_element_type=jnp.float32
        )
        sums = sums[: power.shape[0]] + sums[power.shape[0] :]
        span = stations * time_blocks
        energy = sums[:span, :BLK] + sums[stations * lag_blocks :, BLK : 2 * BLK]
        for b in range(1, lag_blocks):
            energy = energy + sums[stations * b : stations * b + span, 2 * BLK :]
        inverse = 1.0 / jnp.sqrt(energy)
        return [
            [jnp.broadcast_to(inverse[stations * b + s : stations * b + s + 1], (ROWS, BLK)) for b in range(time_blocks)]
            for s in range(stations)
        ]

    tall = 16
    pairs = lag_blocks // 2
    time_pairs = time_blocks // 2

    def hankel(filtered, low, high, s):
        at = lax.broadcasted_iota(jnp.int32, (tall, BLK), 0) + lax.broadcasted_iota(jnp.int32, (tall, BLK), 1)
        lane = lax.broadcasted_iota(jnp.int32, (tall, BLK), 1)
        turned = [
            lane_gather(
                jnp.broadcast_to(filtered[stations * c + s : stations * c + s + 1, :], (tall, BLK)), at & (BLK - 1)
            )
            for c in range(high + 1 - low)
        ]
        heads = [
            jnp.where(at < BLK, turned[c], turned[min(c + 1, high - low)]).astype(jnp.bfloat16)
            for c in range(high + 1 - low)
        ]
        return {
            low + c: jnp.concatenate(
                [heads[c]]
                + [
                    pltpu.roll(jnp.where(lane < q, heads[c + 1], heads[c]), BLK - q, 1)
                    for q in range(tall, BLK, tall)
                ],
                axis=0,
            )
            for c in range(high - low)
        }

    def products(blocks, low, high, s, raw):
        raw = list(raw)
        for c in range(low, high):
            tile = jnp.concatenate(
                [
                    jnp.concatenate([blocks[2 * c], blocks[2 * c + 1]], axis=1),
                    jnp.concatenate([blocks[2 * c + 1], blocks[2 * c + 2]], axis=1),
                ],
                axis=0,
            )
            used = [p for p in range(time_pairs) if 0 <= c - p < pairs]
            first = pairs - 1 - (c - used[0])
            rows = tpl_split[s, first : first + len(used)].reshape(len(used) * n_rows, 2 * BLK)
            product = jnp.dot(rows, tile, preferred_element_type=jnp.float32)
            for i, p in enumerate(used):
                part = product[i * n_rows : (i + 1) * n_rows]
                raw[p] = part if raw[p] is None else raw[p] + part
        for p in range(time_pairs):
            raw_buf[s, p] = raw[p]

    row_lane = lax.broadcasted_iota(jnp.int32, (ROWS, BLK), 1)

    def shift(top, scales):
        halves = []
        for at in (top, top + ROWS):
            stack = [None] * out_blocks
            for s in range(stations):
                moved = moved_ref[s, at : at + ROWS]
                weight = weight_ref[s, at : at + ROWS]
                index = (row_lane + moved) & (BLK - 1)
                stay = row_lane >= moved
                scaled = [
                    raw_buf[s, b // 2, at : at + ROWS, (b % 2) * BLK : (b % 2 + 1) * BLK] * scales[s][b]
                    for b in range(time_blocks)
                ]
                for b in range(out_blocks):
                    term = weight * lane_gather(jnp.where(stay, scaled[b], scaled[b + 1]), index)
                    stack[b] = term if stack[b] is None else stack[b] + term
            halves.append(jnp.concatenate(stack, axis=1))
        rows = jnp.concatenate(halves, axis=0).astype(jnp.bfloat16)
        send_buf[top // own_rows : (top + 2 * ROWS) // own_rows] = rows.reshape(
            2 * ROWS // own_rows, own_rows, out_blocks * BLK
        )

    def of_planes(planes):
        return [
            top
            for top in range(0, n_rows, 2 * ROWS)
            if any(
                owner % (dims[1] * dims[2]) // dims[2] in planes
                for owner in range(top // own_rows, (top + 2 * ROWS - 1) // own_rows + 1)
            )
        ]

    waves = [early[:2], early[2:], late]
    tops = [of_planes(planes) for planes in waves]
    tops[1] = [top for top in tops[1] if top not in tops[0]]
    tops[2] = [top for top in tops[2] if top not in tops[0] + tops[1]]

    def rest(low, before):
        start = 2 * low
        filtered = filter_blocks(0 if low == 0 else start + 2, wave_blocks)
        if low:
            filtered = jnp.concatenate([before, filtered], axis=0)
        scales = scales_of(filtered)
        for s in range(stations):
            if low:
                blocks = hankel(filtered[stations * (start + 1) :], start + 1, wave_blocks - 1, s)
                blocks[start] = edge_buf[s]
            else:
                blocks = hankel(filtered, 0, wave_blocks - 1, s)
            products(
                blocks,
                low,
                pairs + time_pairs - 1,
                s,
                [raw_buf[s, p] for p in range(time_pairs)] if low else [None] * time_pairs,
            )
        for s in range(stations):
            for b in range(time_blocks):
                scale_buf[s, b] = scales[s][b]
        for top in tops[0]:
            shift(top, scales)

    near_blocks = wave_blocks // 2
    near_pairs = (near_blocks - 2) // 2
    in_first = me_t < half
    wave_wait(0)

    @pl.when(in_first)
    def _():
        filtered = filter_blocks(0, near_blocks)
        filtered_buf[...] = filtered
        for s in range(stations):
            blocks = hankel(filtered, 0, near_blocks - 1, s)
            products(blocks, 0, near_pairs, s, [None] * time_pairs)
            edge_buf[s] = blocks[2 * near_pairs]

    wave_wait(1)
    wave_wait(2)

    @pl.when(in_first)
    def _():
        rest(near_pairs, filtered_buf[...])

    @pl.when(jnp.logical_not(in_first))
    def _():
        rest(0, None)

    def send(to):
        pltpu.make_async_remote_copy(
            src_ref=send_buf.at[to],
            dst_ref=recv_buf.at[me_s],
            send_sem=stack_send,
            recv_sem=stack_recv,
            device_id={"sta": to},
            device_id_type=MESH,
        ).start()

    scales = [[scale_buf[s, b] for b in range(time_blocks)] for s in range(stations)]
    each(waves[0], send)
    for top in tops[1]:
        shift(top, scales)
    each(waves[1], send)
    for top in tops[2]:
        shift(top, scales)
    recv_buf[me_s] = send_buf[me_s]

    @pl.when(is_early)
    def _():
        pl.semaphore_wait(chain_sem.at[0], len(plane) * len(late))
        for at in late:
            @pl.when(me_z == nearest(at, early, dims[1]))
            def _():
                tell(chain_sem.at[1], place(0, 0, at))

    @pl.when(jnp.logical_not(is_early))
    def _():
        pl.semaphore_wait(chain_sem.at[1], 1)

    each(late, send)
    arrived = recv_buf.at[pl.ds(0, n_sta - 1)]
    pltpu.make_async_copy(arrived, arrived, stack_recv).wait()
    for copy in wave_copies:
        copy.wait_send()
    pltpu.make_async_copy(arrived, arrived, stack_send).wait()


def add_kernel(parts_ref, out_ref):
    out_ref[0] = jnp.sum(parts_ref[...].astype(jnp.float32), axis=0)


def shards(n_sta, n_tpl, waveform, fir_taps, templates, presence, moveout):
    stations, segment = waveform.shape
    n_rows, _, lags = templates.shape
    own_rows = n_rows // n_sta
    out_len = segment * n_tpl - lags - SHIFT_MOST
    lag_blocks = lags // BLK
    time_pairs = (segment * n_tpl // BLK - lag_blocks) // 2
    hbm = pl.BlockSpec(memory_space=pl.ANY)
    vmem = pl.BlockSpec(memory_space=pltpu.VMEM)
    parts = pl.pallas_call(
        functools.partial(kernel, n_sta, n_tpl),
        out_shape=pltpu.VMEM((n_sta, own_rows, out_len), jnp.bfloat16),
        in_specs=[hbm] * 5,
        out_specs=vmem,
        scratch_shapes=[
            pltpu.VMEM((n_tpl, stations, segment), jnp.float32),
            pltpu.VMEM((lag_blocks, n_rows, stations, BLK), jnp.bfloat16),
            pltpu.VMEM((2, n_rows * stations, BLK), jnp.float32),
            pltpu.VMEM((stations, lag_blocks // 2, n_rows, 2 * BLK), jnp.bfloat16),
            pltpu.VMEM((stations, time_pairs, n_rows, 2 * BLK), jnp.float32),
            pltpu.VMEM((stations * segment * n_tpl // (2 * BLK), BLK), jnp.float32),
            pltpu.VMEM((stations, BLK, BLK), jnp.bfloat16),
            pltpu.VMEM((stations, 2 * time_pairs, ROWS, BLK), jnp.float32),
            pltpu.VMEM((stations, n_rows, BLK), jnp.int32),
            pltpu.VMEM((stations, n_rows, BLK), jnp.float32),
            pltpu.VMEM((n_sta, own_rows, out_len), jnp.bfloat16),
            pltpu.VMEM((2 * BLK, 3 * BLK), jnp.bfloat16),
            pltpu.VMEM((1, fir_taps.shape[0]), jnp.float32),
            pltpu.VMEM((stations, n_rows), jnp.int32),
            pltpu.VMEM((stations, n_rows), jnp.int32),
            pltpu.SemaphoreType.DMA((1 + lag_blocks,)),
            pltpu.SemaphoreType.DMA((3,)),
            pltpu.SemaphoreType.REGULAR((2,)),
            pltpu.SemaphoreType.DMA((n_tpl - 1,)),
            pltpu.SemaphoreType.DMA((n_tpl - 1,)),
            pltpu.SemaphoreType.DMA,
            pltpu.SemaphoreType.DMA,
        ],
        compiler_params=pltpu.CompilerParams(
            collective_id=0, has_side_effects=True
        ),
    )(waveform, fir_taps[None, :], templates, presence.T, moveout.T)
    return pl.pallas_call(
        add_kernel,
        out_shape=jax.ShapeDtypeStruct((1, own_rows, out_len), jnp.float32),
        in_specs=[vmem],
        out_specs=vmem,
    )(pltpu.with_memory_space_constraint(parts, pltpu.VMEM))


def solution(mesh):
    placed = (P("sta", "tpl"), P(), P("tpl", "sta", None), P("tpl", "sta"), P("tpl", "sta"))
    return jax.shard_map(
        functools.partial(shards, mesh.shape["sta"], mesh.shape["tpl"]),
        mesh=mesh,
        in_specs=placed,
        out_specs=P("tpl", "sta", None),
        check_vma=False,
    )
```

profile of v0, /device:TPU:1, one launch (start us, length us, event | category | flops | bytes accessed | tf_op | source)
XLA Modules:
  0.0 19.4 jit_solution(6814333401428128862)
XLA Ops:
  0.0 18.7 %shard_map.55.parts_ref = bf16[64,2,384]{2,1,0:T(2,128)(2,1)S(1)} custom-call(f32[2,384]{1,0:T(2,128)} %wave_ref.1, f32[1,64]{1,0:T(1,128)} %bitcast.5, bf16[128,2,1024]{2,1,0:T(2,128)(2,1)} %tpl_ref.1, s32[2,128]{1,0:T(2,128)} %bitcast.3, s32[2,128]{1,0:T(2,128)} %bitcast.4), custom_call_target="tpu_custom_call" | custom-call | tf_op jit(solution)/shard_map/pallas_call | solution.py:430
  18.7 0.7 %shard_map.56 = f32[1,2,384]{2,1,0:T(2,128)} custom-call(bf16[64,2,384]{2,1,0:T(2,128)(2,1)S(1)} %shard_map.55.parts_ref), custom_call_target="tpu_custom_call" | custom-call | tf_op jit(solution)/shard_map/pallas_call | solution.py:463
where the time goes:
time: 19.5 us; the launch traced here: 19.4 us
  Pallas kernels  19.4 us (99%)
    pallas_call x1, Pallas kernels, shards(): pl.pallas_call(functools.partial(kernel, n_sta, n_tpl), out_shape=pltpu.V...  18.7 us
    pallas_call x1, Pallas kernels, shards(): pl.pallas_call(add_kernel, out_shape=jax.ShapeDtypeStruct((1, own_rows, o...  0.68 us

commit v1 on v0

--- a/solution.py
+++ b/solution.py
@@ -266,8 +266,13 @@
             for c in range(high - low)
         }
 
-    def products(blocks, low, high, s, raw):
-        raw = list(raw)
+    def products(blocks, low, high, s, tops, add):
+        raw = [None] * time_pairs
+        if add:
+            raw = [
+                jnp.concatenate([raw_buf[s, p, top : top + 2 * ROWS] for top in tops], axis=0) for p in range(time_pairs)
+            ]
+        count = len(tops) * 2 * ROWS
         for c in range(low, high):
             tile = jnp.concatenate(
                 [
@@ -277,14 +282,16 @@
                 axis=0,
             )
             used = [p for p in range(time_pairs) if 0 <= c - p < pairs]
-            first = pairs - 1 - (c - used[0])
-            rows = tpl_split[s, first : first + len(used)].reshape(len(used) * n_rows, 2 * BLK)
+            rows = jnp.concatenate(
+                [tpl_split[s, pairs - 1 - (c - p), top : top + 2 * ROWS] for p in used for top in tops], axis=0
+            )
             product = jnp.dot(rows, tile, preferred_element_type=jnp.float32)
             for i, p in enumerate(used):
-                part = product[i * n_rows : (i + 1) * n_rows]
+                part = product[i * count : (i + 1) * count]
                 raw[p] = part if raw[p] is None else raw[p] + part
         for p in range(time_pairs):
-            raw_buf[s, p] = raw[p]
+            for i, top in enumerate(tops):
+                raw_buf[s, p, top : top + 2 * ROWS] = raw[p][i * 2 * ROWS : (i + 1) * 2 * ROWS]
 
     row_lane = lax.broadcasted_iota(jnp.int32, (ROWS, BLK), 1)
 
@@ -325,56 +332,6 @@
     tops[1] = [top for top in tops[1] if top not in tops[0]]
     tops[2] = [top for top in tops[2] if top not in tops[0] + tops[1]]
 
-    def rest(low, before):
-        start = 2 * low
-        filtered = filter_blocks(0 if low == 0 else start + 2, wave_blocks)
-        if low:
-            filtered = jnp.concatenate([before, filtered], axis=0)
-        scales = scales_of(filtered)
-        for s in range(stations):
-            if low:
-                blocks = hankel(filtered[stations * (start + 1) :], start + 1, wave_blocks - 1, s)
-                blocks[start] = edge_buf[s]
-            else:
-                blocks = hankel(filtered, 0, wave_blocks - 1, s)
-            products(
-                blocks,
-                low,
-                pairs + time_pairs - 1,
-                s,
-                [raw_buf[s, p] for p in range(time_pairs)] if low else [None] * time_pairs,
-            )
-        for s in range(stations):
-            for b in range(time_blocks):
-                scale_buf[s, b] = scales[s][b]
-        for top in tops[0]:
-            shift(top, scales)
-
-    near_blocks = wave_blocks // 2
-    near_pairs = (near_blocks - 2) // 2
-    in_first = me_t < half
-    wave_wait(0)
-
-    @pl.when(in_first)
-    def _():
-        filtered = filter_blocks(0, near_blocks)
-        filtered_buf[...] = filtered
-        for s in range(stations):
-            blocks = hankel(filtered, 0, near_blocks - 1, s)
-            products(blocks, 0, near_pairs, s, [None] * time_pairs)
-            edge_buf[s] = blocks[2 * near_pairs]
-
-    wave_wait(1)
-    wave_wait(2)
-
-    @pl.when(in_first)
-    def _():
-        rest(near_pairs, filtered_buf[...])
-
-    @pl.when(jnp.logical_not(in_first))
-    def _():
-        rest(0, None)
-
     def send(to):
         pltpu.make_async_remote_copy(
             src_ref=send_buf.at[to],
@@ -385,8 +342,56 @@
             device_id_type=MESH,
         ).start()
 
+    def rest(low, before):
+        start = 2 * low
+        filtered = filter_blocks(0 if low == 0 else start + 2, wave_blocks)
+        if low:
+            filtered = jnp.concatenate([before, filtered], axis=0)
+        scales = scales_of(filtered)
+        blocks = []
+        for s in range(stations):
+            if low:
+                blocks.append(hankel(filtered[stations * (start + 1) :], start + 1, wave_blocks - 1, s))
+                blocks[s][start] = edge_buf[s]
+            else:
+                blocks.append(hankel(filtered, 0, wave_blocks - 1, s))
+        for s in range(stations):
+            products(blocks[s], low, pairs + time_pairs - 1, s, tops[0], low > 0)
+        for s in range(stations):
+            for b in range(time_blocks):
+                scale_buf[s, b] = scales[s][b]
+        for top in tops[0]:
+            shift(top, scales)
+        each(waves[0], send)
+        for s in range(stations):
+            products(blocks[s], low, pairs + time_pairs - 1, s, tops[1] + tops[2], low > 0)
+
+    near_blocks = wave_blocks // 2
+    near_pairs = (near_blocks - 2) // 2
+    in_first = me_t < half
+    wave_wait(0)
+
+    @pl.when(in_first)
+    def _():
+        filtered = filter_blocks(0, near_blocks)
+        filtered_buf[...] = filtered
+        for s in range(stations):
+            blocks = hankel(filtered, 0, near_blocks - 1, s)
+            products(blocks, 0, near_pairs, s, sum(tops, []), False)
+            edge_buf[s] = blocks[2 * near_pairs]
+
+    wave_wait(1)
+    wave_wait(2)
+
+    @pl.when(in_first)
+    def _():
+        rest(near_pairs, filtered_buf[...])
+
+    @pl.when(jnp.logical_not(in_first))
+    def _():
+        rest(0, None)
+
     scales = [[scale_buf[s, b] for b in range(time_blocks)] for s in range(stations)]
-    each(waves[0], send)
     for top in tops[1]:
         shift(top, scales)
     each(waves[1], send)

time: 19.5 us -> 19.3 us (0.990)
  Pallas kernels: 19.4 us -> 19.2 us
where the time goes in v1:
time: 19.3 us; the launch traced here: 19.2 us
  Pallas kernels  19.2 us (99%)
    pallas_call x1, Pallas kernels, shards(): pl.pallas_call(functools.partial(kernel, n_sta, n_tpl), out_shape=pltpu.V...  18.5 us
    pallas_call x1, Pallas kernels, shards(): pl.pallas_call(add_kernel, out_shape=jax.ShapeDtypeStruct((1, own_rows, o...  0.68 us

profile of v1, /device:TPU:1, one launch (start us, length us, event | category | flops | bytes accessed | tf_op | source)
XLA Modules:
  0.0 19.2 jit_solution(13458584313077023702)
XLA Ops:
  0.0 18.5 %shard_map.55.parts_ref = bf16[64,2,384]{2,1,0:T(2,128)(2,1)S(1)} custom-call(f32[2,384]{1,0:T(2,128)} %wave_ref.1, f32[1,64]{1,0:T(1,128)} %bitcast.5, bf16[128,2,1024]{2,1,0:T(2,128)(2,1)} %tpl_ref.1, s32[2,128]{1,0:T(2,128)} %bitcast.3, s32[2,128]{1,0:T(2,128)} %bitcast.4), custom_call_target="tpu_custom_call" | custom-call | tf_op jit(solution)/shard_map/pallas_call | solution.py:435
  18.5 0.7 %shard_map.56 = f32[1,2,384]{2,1,0:T(2,128)} custom-call(bf16[64,2,384]{2,1,0:T(2,128)(2,1)S(1)} %shard_map.55.parts_ref), custom_call_target="tpu_custom_call" | custom-call | tf_op jit(solution)/shard_map/pallas_call | solution.py:468

commit v2 on v1

--- a/solution.py
+++ b/solution.py
@@ -355,7 +355,6 @@
                 blocks[s][start] = edge_buf[s]
             else:
                 blocks.append(hankel(filtered, 0, wave_blocks - 1, s))
-        for s in range(stations):
             products(blocks[s], low, pairs + time_pairs - 1, s, tops[0], low > 0)
         for s in range(stations):
             for b in range(time_blocks):
@@ -417,10 +416,6 @@
     for copy in wave_copies:
         copy.wait_send()
     pltpu.make_async_copy(arrived, arrived, stack_send).wait()
-
-
-def add_kernel(parts_ref, out_ref):
-    out_ref[0] = jnp.sum(parts_ref[...].astype(jnp.float32), axis=0)
 
 
 def shards(n_sta, n_tpl, waveform, fir_taps, templates, presence, moveout):
@@ -465,12 +460,7 @@
             collective_id=0, has_side_effects=True
         ),
     )(waveform, fir_taps[None, :], templates, presence.T, moveout.T)
-    return pl.pallas_call(
-        add_kernel,
-        out_shape=jax.ShapeDtypeStruct((1, own_rows, out_len), jnp.float32),
-        in_specs=[vmem],
-        out_specs=vmem,
-    )(pltpu.with_memory_space_constraint(parts, pltpu.VMEM))
+    return jnp.sum(parts.astype(jnp.float32), axis=0)[None]
 
 
 def solution(mesh):

time: 19.3 us -> 19.3 us (level)
  Pallas kernels: 19.2 us -> 18.5 us
  other arithmetic: 0 us -> 0.69 us
    reduce_sum x0 -> x1, other arithmetic: none -> 0.69 us  [shards(): return jnp.sum(parts.astype(jnp.float32), axis=0)[None]]
    pallas_call x1 -> x0, Pallas kernels: 0.68 us -> none  [shards(): pl.pallas_call(add_kernel, out_shape=jax.ShapeDtypeStruct((1, own_rows, o...]
where the time goes in v2:
time: 19.3 us; the launch traced here: 19.2 us
  Pallas kernels  18.5 us (96%)
  other arithmetic  0.69 us (4%)
    pallas_call x1, Pallas kernels, shards(): pl.pallas_call(functools.partial(kernel, n_sta, n_tpl), out_shape=pltpu.V...  18.5 us
    reduce_sum x1, other arithmetic, shards(): return jnp.sum(parts.astype(jnp.float32), axis=0)[None]  0.69 us

profile of v2, /device:TPU:1, one launch (start us, length us, event | category | flops | bytes accessed | tf_op | source)
XLA Modules:
  0.0 19.2 jit_solution(6833682251212984121)
XLA Ops:
  0.0 18.5 %shard_map.55 = bf16[64,2,384]{2,1,0:T(2,128)(2,1)S(1)} custom-call(f32[2,384]{1,0:T(2,128)} %wave_ref.1, f32[1,64]{1,0:T(1,128)} %bitcast.6, bf16[128,2,1024]{2,1,0:T(2,128)(2,1)} %tpl_ref.1, s32[2,128]{1,0:T(2,128)} %bitcast.4, s32[2,128]{1,0:T(2,128)} %bitcast.5), custom_call_target="tpu_custom_call" | custom-call | tf_op jit(solution)/shard_map/pallas_call | solution.py:430
  18.5 0.7 %convert_reduce_fusion = f32[2,384]{1,0:T(2,128)} fusion(bf16[64,2,384]{2,1,0:T(2,128)(2,1)S(1)} %shard_map.55), kind=kLoop, calls=%fused_computation | loop fusion | flops 97536 | bytes 101376 | tf_op jit(solution)/shard_map/reduce_sum | solution.py:463

commit v3 on v1

--- a/solution.py
+++ b/solution.py
@@ -347,7 +347,6 @@
         filtered = filter_blocks(0 if low == 0 else start + 2, wave_blocks)
         if low:
             filtered = jnp.concatenate([before, filtered], axis=0)
-        scales = scales_of(filtered)
         blocks = []
         for s in range(stations):
             if low:
@@ -357,6 +356,7 @@
                 blocks.append(hankel(filtered, 0, wave_blocks - 1, s))
         for s in range(stations):
             products(blocks[s], low, pairs + time_pairs - 1, s, tops[0], low > 0)
+        scales = scales_of(filtered)
         for s in range(stations):
             for b in range(time_blocks):
                 scale_buf[s, b] = scales[s][b]

time: 19.3 us -> 19.4 us (level)
  no operation moved by 1% of the time
where the time goes in v3:
time: 19.4 us; the launch traced here: 19.3 us
  Pallas kernels  19.3 us (99%)
    pallas_call x1, Pallas kernels, shards(): pl.pallas_call(functools.partial(kernel, n_sta, n_tpl), out_shape=pltpu.V...  18.6 us
    pallas_call x1, Pallas kernels, shards(): pl.pallas_call(add_kernel, out_shape=jax.ShapeDtypeStruct((1, own_rows, o...  0.68 us

profile of v3, /device:TPU:1, one launch (start us, length us, event | category | flops | bytes accessed | tf_op | source)
XLA Modules:
  0.0 19.3 jit_solution(13582007417168853558)
XLA Ops:
  0.0 18.6 %shard_map.55.parts_ref = bf16[64,2,384]{2,1,0:T(2,128)(2,1)S(1)} custom-call(f32[2,384]{1,0:T(2,128)} %wave_ref.1, f32[1,64]{1,0:T(1,128)} %bitcast.5, bf16[128,2,1024]{2,1,0:T(2,128)(2,1)} %tpl_ref.1, s32[2,128]{1,0:T(2,128)} %bitcast.3, s32[2,128]{1,0:T(2,128)} %bitcast.4), custom_call_target="tpu_custom_call" | custom-call | tf_op jit(solution)/shard_map/pallas_call | solution.py:435
  18.6 0.7 %shard_map.56 = f32[1,2,384]{2,1,0:T(2,128)} custom-call(bf16[64,2,384]{2,1,0:T(2,128)(2,1)S(1)} %shard_map.55.parts_ref), custom_call_target="tpu_custom_call" | custom-call | tf_op jit(solution)/shard_map/pallas_call | solution.py:468
